TPU v7x, 32 devices: a whole 2x2x4 slice. The times are simulated.
32 devices in a mesh: mp: 2 (over core), feat: 16 (over z, y, x).
Axes of the slice: x: 2, y: 2, z: 4, core: 2. Of those that a mesh axis runs over, the one named last changes fastest.
Arguments:
- residual: bfloat16 [2, 96, 2304], P(None, 'feat', 'mp'), may hold values from -6 to 6
- norm_gain: float32 [2, 2304], P(None, 'mp'), may hold values from 0.1 to 1.9
- gate_weight: bfloat16 [2, 2304, 9216], P(None, 'mp', 'feat'), may hold values from -0.125 to 0.125
- up_weight: bfloat16 [2, 2304, 9216], P(None, 'mp', 'feat'), may hold values from -0.125 to 0.125
- down_weight: bfloat16 [2, 9216, 2304], P(None, 'feat', 'mp'), may hold values from -0.0625 to 0.0625
- encoder: bfloat16 [2, 32768, 2304], P(None, 'feat', 'mp'), may hold values from -0.125 to 0.125
- encoder_bias: float32 [2, 32768], P(None, 'feat'), may hold values from -3 to 3
- decoder: bfloat16 [3, 32768, 2304], P(None, 'feat', 'mp'), may hold values from -0.03125 to 0.03125
Outputs:
- grad_encoder: bfloat16 [2, 32768, 2304], P(None, 'feat', 'mp')
- grad_bias: float32 [2, 32768], P(None, 'feat')
- grad_decoder: bfloat16 [3, 32768, 2304], P(None, 'feat', 'mp')
All inputs are finite; a program needn't handle non-finite values.
Results may differ from a plain program's by a relative error of at most 0.02.
The roundings to bfloat16 on the way count: a program that leaves them out, or rounds other values in their place, can miss the bound.
Values may be sent and summed in bfloat16 or wider, within the bound.
No kernel may reach another device: no remote copies, remote signals or barrier semaphores. Data moves between devices by JAX's collectives and lax.ppermute only.
A program may use at most 128 MiB of HBM per device.

v0:
```python
import math
import jax
import jax.numpy as jnp
from jax import lax
from jax.sharding import PartitionSpec as P

D = 2304
sparsity_weight = 0.1


def outer_product(weights_side, errors_side):
    return lax.dot_general(
        weights_side, errors_side, (((0,), (0,)), ((), ())), preferred_element_type=jnp.float32
    )


def body(residual, norm_gain, gate_weight, up_weight, down_weight, encoder, encoder_bias, decoder):
    values = residual.astype(jnp.float32)
    squares = lax.psum(jnp.sum(values * values, axis=2), "mp")
    inverse_rms = lax.rsqrt(squares / D + 1e-06)
    normed_local = (values * inverse_rms[:, :, None] * norm_gain[:, None, :]).astype(jnp.bfloat16)
    normed = lax.all_gather(normed_local, "feat", axis=1, tiled=True)
    tokens = normed.shape[1]
    local_rows = residual.shape[1]
    gate_part = jnp.einsum("ltd,ldh->lth", normed, gate_weight, preferred_element_type=jnp.float32)
    up_part = jnp.einsum("ltd,ldh->lth", normed, up_weight, preferred_element_type=jnp.float32)
    gate_part, up_part = (
        lax.psum(gate_part.astype(jnp.bfloat16), "mp").astype(jnp.float32),
        lax.psum(up_part.astype(jnp.bfloat16), "mp").astype(jnp.float32),
    )
    hidden = (jax.nn.gelu(gate_part, approximate=True) * up_part).astype(jnp.bfloat16)
    preact_part = jnp.einsum("ltd,lfd->tlf", normed, encoder, preferred_element_type=jnp.float32)
    preact = lax.psum(preact_part, "mp")
    active = jnp.maximum(preact + encoder_bias[None], 0.0).astype(jnp.bfloat16)
    features = active.shape[2]
    model_cols = decoder.shape[2]
    joined = jnp.concatenate([decoder[1], decoder[2]], axis=0)
    picked = hidden
    partial_value = jnp.einsum(
        "lth,lhd->tld", picked, down_weight, preferred_element_type=jnp.float32
    )
    picked = active
    first_part = jnp.dot(picked[:, 0], decoder[0], preferred_element_type=jnp.float32)
    second = jnp.dot(
        picked.reshape(local_rows * lax.axis_size("feat"), 2 * features),
        joined,
        preferred_element_type=jnp.float32,
    )
    errors_local = lax.psum_scatter(
        jnp.concatenate([first_part, second], axis=1)
        - partial_value.reshape(local_rows * lax.axis_size("feat"), -1),
        "feat",
        scatter_dimension=0,
        tiled=True,
    ).astype(jnp.bfloat16)
    errors = lax.all_gather(errors_local, "feat", axis=0, tiled=True)
    error_first = errors[:, :model_cols]
    error_second = errors[:, model_cols:]
    first_rows = jnp.concatenate([decoder[0], decoder[1]], axis=1)
    back_first = lax.dot_general(
        errors, first_rows, (((1,), (1,)), ((), ())), preferred_element_type=jnp.float32
    )
    back_second = lax.dot_general(
        error_second, decoder[2], (((1,), (1,)), ((), ())), preferred_element_type=jnp.float32
    )
    back_stack = jnp.stack([back_first, back_second], axis=1)
    loss_scale = 1.0 / math.sqrt(tokens)
    backward = lax.psum(back_stack.astype(jnp.bfloat16), "mp").astype(jnp.float32)
    pre_grad = jnp.where(active > 0, loss_scale * (backward + sparsity_weight), 0.0).astype(
        jnp.bfloat16
    )
    grad_encoder = jnp.einsum(
        "tlf,ltd->lfd", pre_grad, normed, preferred_element_type=jnp.float32
    ).astype(jnp.bfloat16)
    grad_bias = jnp.sum(pre_grad.astype(jnp.float32), axis=0)
    active_first = active[:, 0]
    active_second = active[:, 1]
    grad_decoder = (
        loss_scale
        * jnp.stack(
            [
                outer_product(active_first, error_first),
                outer_product(active_first, error_second),
                outer_product(active_second, error_second),
            ]
        )
    ).astype(jnp.bfloat16)
    return (grad_encoder, grad_bias, grad_decoder)


def solution(mesh):
    return jax.shard_map(
        body,
        mesh=mesh,
        in_specs=(
            P(None, "feat", "mp"),
            P(None, "mp"),
            P(None, "mp", "feat"),
            P(None, "mp", "feat"),
            P(None, "feat", "mp"),
            P(None, "feat", "mp"),
            P(None, "feat"),
            P(None, "feat", "mp"),
        ),
        out_specs=(P(None, "feat", "mp"), P(None, "feat"), P(None, "feat", "mp")),
        check_vma=False,
    )
```

profile of v0, /device:TPU:0, one launch (start us, length us, event | category | flops | bytes accessed | tf_op | source)
XLA Modules:
  0.0 270.2 jit_solution(11253927287694514613)
XLA Ops:
  7.2 0.0 copy-start
  7.2 0.0 all-reduce.11.cloned.1.call-start
  7.2 1.0 fusion.38
  8.2 2.6 psum.35
  10.9 0.8 fusion.40
  11.7 44.8 %all_gather.6 = bf16[2,96,1152]{2,0,1:T(2,128)(2,1)S(1)} all-gather(bf16[2,6,1152]{2,0,1:T(2,128)(2,1)S(1)} %fusion.40), channel_id=1, replica_groups=mesh['mp'=2,'feat'=16] {'feat'}, dimensions={1}, use_global_device_ids=true | all-gather | bytes 470016 | tf_op jit(solution)/shard_map/all_gather | solution.py:22
  56.5 3.6 %convolution_convert_fusion.3 = bf16[2,96,576]{2,1,0:T(8,128)(2,1)} fusion(bf16[2,1152,576]{1,2,0:T(8,128)(2,1)} %param.10, bf16[2,96,1152]{2,0,1:T(2,128)(2,1)S(1)} %all_gather.6), kind=kOutput, calls=%fused_computation.27 | convolution fusion | flops 254914560 | bytes 3317760 | tf_op jit(solution)/shard_map/ltd,ldh->lth/dot_general | solution.py:25
  60.1 3.4 %convolution_convert_fusion.2 = bf16[2,96,576]{2,1,0:T(8,128)(2,1)} fusion(bf16[2,1152,576]{1,2,0:T(8,128)(2,1)} %param.11, bf16[2,96,1152]{2,0,1:T(2,128)(2,1)S(1)} %all_gather.6), kind=kOutput, calls=%fused_computation.26 | convolution fusion | flops 254914560 | bytes 3317760 | tf_op jit(solution)/shard_map/ltd,ldh->lth/dot_general | solution.py:26
  63.5 0.0 all-reduce.11.cloned.1.call-update
  63.5 0.0 all-reduce.7.cloned.1.call-start
  63.6 8.0 %convolution_bitcast_fusion.4 = f32[96,2,2048]{2,0,1:T(8,128)} fusion(bf16[2,2048,1152]{2,1,0:T(8,128)(2,1)} %param.13, bf16[2,96,1152]{2,0,1:T(2,128)(2,1)S(1)} %all_gather.6), kind=kOutput, calls=%fused_computation.18 | convolution fusion | flops 905969664 | bytes 11452416 | tf_op jit(solution)/shard_map/ltd,lfd->tlf/dot_general | solution.py:32
  71.6 0.0 all-reduce.7.cloned.1.call-update
  71.6 0.0 all-reduce.9.cloned.1.call-start
  71.7 11.3 %slice_bitcast_fusion.2 = (bf16[2048,1152]{1,0:T(8,128)(2,1)}, bf16[2048,1152]{1,0:T(8,128)(2,1)}, bf16[2048,1152]{1,0:T(8,128)(2,1)}) fusion(bf16[3,2048,1152]{2,1,0:T(8,128)(2,1)} %param.15), kind=kLoop, calls=%fused_computation.16 | loop fusion | bytes 28311552 | tf_op jit(solution)/shard_map/squeeze | solution.py:43
  83.0 1.7 convolution_bitcast_fusion.3
  84.7 0.1 copy.23
  84.8 17.4 %all-reduce.7.cloned.1.call-done = f32[96,2,2048]{2,0,1:T(8,128)} async-done(((f32[96,2,2048]{2,0,1:T(8,128)}), f32[96,2,2048]{2,0,1:T(8,128)}) %all-reduce.7.cloned.1.call-update) | async-done | bytes 1572880 | tf_op jit(solution)/shard_map/psum | solution.py:33
  102.1 1.7 maximum_convert_fusion
  103.9 0.0 slice-start.3
  103.9 0.0 copy-start.4
  103.9 3.7 %fusion.24 = f32[96,1152]{1,0:T(8,128)S(1)} fusion(bf16[96,2,2048]{2,0,1:T(8,128)(2,1)S(1)} %maximum_convert_fusion, bf16[3,2048,1152]{2,1,0:T(8,128)(2,1)} %param.15), kind=kOutput, calls=%fused_computation.43 | convolution fusion | flops 452984832 | bytes 5554176 | tf_op jit(solution)/shard_map/dot_general | solution.py:43
  107.6 0.2 fusion.59
  107.8 0.1 copy.22
  107.9 0.6 copy-done.4
  108.5 2.0 fusion.2
  110.5 0.1 maximum_subtract_fusion
  110.6 49.0 %fusion = f32[8,2304]{1,0:T(8,128)S(1)} fusion(f32[96,2304]{1,0:T(8,128)S(1)} %maximum_subtract_fusion), kind=kCustom, calls=%all-reduce-scatter | all-reduce-scatter fusion | flops 294913 | bytes 958976
  159.6 1.3 collective-permute-start.1
  160.9 1.3 collective-permute-start.2
  162.2 1.9 collective-permute-start
  164.1 2.4 collective-permute-start.3
  166.5 0.6 dynamic-slice.4
  167.8 0.4 collective-permute-done.3
  168.1 0.0 collective-permute-done.1
  168.1 0.0 collective-permute-done
  168.1 0.6 concatenate.12
  168.8 43.6 %all-gather = bf16[16,6,2304]{2,1,0:T(8,128)(2,1)S(1)} all-gather(bf16[1,6,2304]{2,1,0:T(8,128)(2,1)S(1)} %fusion.41), channel_id=1, replica_groups=mesh['mp'=2,'feat'=16] {'feat'}, dimensions={0}, use_global_device_ids=true | all-gather | bytes 470016 | tf_op jit(solution)/shard_map/all_gather | solution.py:56
  212.4 0.1 reshape.18
  212.5 3.9 %fusion.16 = bf16[96,1,2048]{2,0,1:T(8,128)(2,1)S(1)} fusion(bf16[96,2304]{1,0:T(8,128)(2,1)S(1)} %reshape.18, bf16[3,2048,1152]{2,1,0:T(8,128)(2,1)} %param.15), kind=kOutput, calls=%fused_computation.22 | convolution fusion | flops 453181440 | bytes 5332992 | tf_op jit(solution)/shard_map/dot_general | solution.py:63
  216.4 5.1 %convolution_bitcast_fusion.1 = f32[1,2048,1152]{2,1,0:T(8,128)} fusion(bf16[96,2,2048]{2,0,1:T(8,128)(2,1)S(1)} %maximum_convert_fusion, bf16[96,2304]{1,0:T(8,128)(2,1)S(1)} %reshape.18), kind=kOutput, calls=%fused_computation.12 | convolution fusion | flops 452984832 | bytes 10051584 | tf_op jit(solution)/shard_map/dot_general | solution.py:12
  221.5 5.8 %convolution_bitcast_fusion = f32[1,2048,1152]{2,1,0:T(8,128)} fusion(bf16[96,2,2048]{2,0,1:T(8,128)(2,1)S(1)} %maximum_convert_fusion, bf16[96,2304]{1,0:T(8,128)(2,1)S(1)} %reshape.18), kind=kOutput, calls=%fused_computation.11 | convolution fusion | flops 452984832 | bytes 10051584 | tf_op jit(solution)/shard_map/dot_general | solution.py:12
  227.3 5.1 %convolution_bitcast_fusion.2 = f32[1,2048,1152]{2,1,0:T(8,128)} fusion(bf16[96,2,2048]{2,0,1:T(8,128)(2,1)S(1)} %maximum_convert_fusion, bf16[96,2304]{1,0:T(8,128)(2,1)S(1)} %reshape.18), kind=kOutput, calls=%fused_computation.13 | convolution fusion | flops 452984832 | bytes 10051584 | tf_op jit(solution)/shard_map/dot_general | solution.py:12
  232.4 3.1 %fusion.13 = bf16[96,1,2048]{2,0,1:T(8,128)(2,1)S(1)} fusion(bf16[96,2304]{1,0:T(8,128)(2,1)S(1)} %reshape.18, bf16[2048,1152]{1,0:T(8,128)(2,1)S(1)} %bitcast.51, bf16[2048,1152]{1,0:T(8,128)(2,1)S(1)} %bitcast.47), kind=kOutput, calls=%fused_computation.21 | convolution fusion | flops 925040640 | bytes 10272768 | tf_op jit(solution)/shard_map/dot_general | solution.py:60
  235.6 1.0 pad_maximum_fusion
  236.5 0.0 all-reduce.9.cloned.1.call-update
  236.5 16.6 %fusion.1 = bf16[3,2048,1152]{2,1,0:T(8,128)(2,1)} fusion(f32[1,2048,1152]{2,1,0:T(8,128)} %convolution_bitcast_fusion, f32[1,2048,1152]{2,1,0:T(8,128)} %convolution_bitcast_fusion.1, f32[1,2048,1152]{2,1,0:T(8,128)} %convolution_bitcast_fusion.2), kind=kLoop, calls=%fused_computation.1 | loop fusion | flops 28311552 | bytes 42467328 | tf_op jit(solution)/shard_map/convert_element_type | solution.py:87
  253.2 2.8 %convert_reduce_fusion = f32[2,2048]{1,0:T(2,128)} fusion(bf16[96,2,2048]{2,0,1:T(8,128)(2,1)} %all-reduce.9.cloned.1.call-done, f32[96,2,2048]{2,0,1:T(8,128)} %all-reduce.7.cloned.1.call-done, f32[2,2048]{1,0:T(2,128)S(1)} %copy-done.5), kind=kLoop, calls=%fused_computation.23 | loop fusion | flops 4321280 | bytes 2392064 | tf_op jit(solution)/shard_map/reduce_sum | solution.py:75
  256.0 7.6 %convolution_convert_fusion = bf16[2,2048,1152]{2,1,0:T(8,128)(2,1)} fusion(bf16[2,96,1152]{2,0,1:T(2,128)(2,1)} %copy-done.3, bf16[96,2,2048]{2,0,1:T(8,128)(2,1)} %all-reduce.9.cloned.1.call-done, bf16[96,2,2048]{2,0,1:T(8,128)(2,1)S(1)} %maximum_convert_fusion), kind=kOutput, calls=%fused_computation.2 | convolution fusion | flops 913047552 | bytes 11452416 | tf_op jit(solution)/shard_map/tlf,ltd->lfd/dot_general | solution.py:72
  (32 shorter events, 0.1 us)
Async XLA Ops:
  7.2 75.8 %copy-start = (bf16[2,576,1152]{2,1,0:T(8,128)(2,1)S(1)}, bf16[2,576,1152]{2,1,0:T(8,128)(2,1)}, u32[]{:S(2)}) copy-start(bf16[2,576,1152]{2,1,0:T(8,128)(2,1)} %param.12) | copy-start | bytes 7962628
  7.2 75.8 %all-reduce.11.cloned.1.call-start = ((), (), s32[]{:S(2)}) async-start(), calls=%async_computation.2 | async-start | bytes 983040 | tf_op jit(solution)/shard_map/psum | solution.py:28
  56.5 15.0 %copy-start.3 = (bf16[2,96,1152]{2,0,1:T(2,128)(2,1)}, bf16[2,96,1152]{2,0,1:T(2,128)(2,1)S(1)}, u32[]{:S(2)}) copy-start(bf16[2,96,1152]{2,0,1:T(2,128)(2,1)S(1)} %all_gather.6) | copy-start | bytes 1327108
  63.5 38.6 %all-reduce.7.cloned.1.call-start = ((), (), s32[]{:S(2)}) async-start(), calls=%async_computation | async-start | bytes 3145728 | tf_op jit(solution)/shard_map/psum | solution.py:33
  71.6 181.6 %all-reduce.9.cloned.1.call-start = ((), (), s32[]{:S(2)}) async-start(), calls=%async_computation.1 | async-start | bytes 1572864 | tf_op jit(solution)/shard_map/psum | solution.py:68
  83.0 19.1 %copy-start.5 = (f32[2,2048]{1,0:T(2,128)S(1)}, f32[2,2048]{1,0:T(2,128)}, u32[]{:S(2)}) copy-start(f32[2,2048]{1,0:T(2,128)} %param.14) | copy-start | bytes 49156
  102.1 5.4 %copy-start.2 = (f32[96,2,2048]{2,0,1:T(8,128)S(1)}, f32[96,2,2048]{2,0,1:T(8,128)}, u32[]{:S(2)}) copy-start(f32[96,2,2048]{2,0,1:T(8,128)} %all-reduce.7.cloned.1.call-done) | copy-start | bytes 4718596
  102.1 5.7 %slice-start.2 = ((s8[4718592]{0:T(1024)(128)(4,1)}), s8[4194304]{0:T(1024)(128)(4,1)S(1)}, s32[]{:S(2)}) async-start(s8[4718592]{0:T(1024)(128)(4,1)} %bitcast.48), calls=%async_computation.5 | async-start | bytes 8388608
  103.9 4.0 %slice-start.3 = ((s8[4718592]{0:T(1024)(128)(4,1)}), s8[524288]{0:T(1024)(128)(4,1)S(1)}, s32[]{:S(2)}) async-start(s8[4718592]{0:T(1024)(128)(4,1)} %bitcast.48), calls=%async_computation.6 | async-start | bytes 1048576
  103.9 4.6 %copy-start.4 = (bf16[2048,1152]{1,0:T(8,128)(2,1)S(1)}, bf16[2048,1152]{1,0:T(8,128)(2,1)}, u32[]{:S(2)}) copy-start(bf16[2048,1152]{1,0:T(8,128)(2,1)} %get-tuple-element.6) | copy-start | bytes 14155780
  108.5 58.1 %copy-start.6 = (u32[32]{0:T(128)S(1)}, u32[32]{0:T(128)}, u32[]{:S(2)}) copy-start(u32[32]{0:T(128)} %constant.26) | copy-start | bytes 388
  159.6 8.5 %collective-permute-start.1 = (bf16[8,2304]{1,0:T(8,128)(2,1)S(1)}, bf16[8,2304]{1,0:T(8,128)(2,1)S(1)}, u32[]{:S(2)}, u32[]{:S(2)}) collective-permute-start(bf16[8,2304]{1,0:T(8,128)(2,1)S(1)} %convert.22), channel_id=1, source_target_pairs={{0,2},{1,3},{2,4},{3,5},{4,6},{5,7},{6,8},{7,9},{8,10},{9,11},{10,... | collective-permute-start | bytes 110600
  160.9 7.2 %collective-permute-start.2 = (bf16[8,2304]{1,0:T(8,128)(2,1)S(1)}, bf16[8,2304]{1,0:T(8,128)(2,1)S(1)}, u32[]{:S(2)}, u32[]{:S(2)}) collective-permute-start(bf16[8,2304]{1,0:T(8,128)(2,1)S(1)} %convert.22), channel_id=1, source_target_pairs={{0,3},{1,4},{2,5},{3,6},{4,7},{5,8},{6,9},{7,10},{8,11},{9,12},{10... | collective-permute-start | bytes 110600
  162.2 5.9 %collective-permute-start = (bf16[8,2304]{1,0:T(8,128)(2,1)S(1)}, bf16[8,2304]{1,0:T(8,128)(2,1)S(1)}, u32[]{:S(2)}, u32[]{:S(2)}) collective-permute-start(bf16[8,2304]{1,0:T(8,128)(2,1)S(1)} %convert.22), channel_id=1, source_target_pairs={{0,1},{1,2},{2,3},{3,4},{4,5},{5,6},{6,7},{7,8},{8,9},{9,10},{10,1... | collective-permute-start | bytes 110600
  164.1 4.0 %collective-permute-start.3 = (bf16[6,2304]{1,0:T(8,128)(2,1)S(1)}, bf16[6,2304]{1,0:T(8,128)(2,1)S(1)}, u32[]{:S(2)}, u32[]{:S(2)}) collective-permute-start(bf16[6,2304]{1,0:T(8,128)(2,1)S(1)} %slice.36), channel_id=1, source_target_pairs={{0,4},{1,5},{2,6},{3,7},{4,8},{5,9},{6,10},{7,11},{8,12},{9,13},{1... | collective-permute-start | bytes 82952
  221.5 10.9 %slice-start = ((s8[4718592]{0:T(1024)(128)(4,1)}), s8[4194304]{0:T(1024)(128)(4,1)S(1)}, s32[]{:S(2)}) async-start(s8[4718592]{0:T(1024)(128)(4,1)} %bitcast.46), calls=%async_computation.3 | async-start | bytes 8388608
  221.5 10.9 %slice-start.4 = ((s8[4718592]{0:T(1024)(128)(4,1)}), s8[4194304]{0:T(1024)(128)(4,1)S(1)}, s32[]{:S(2)}) async-start(s8[4718592]{0:T(1024)(128)(4,1)} %bitcast.50), calls=%async_computation.7 | async-start | bytes 8388608
  227.3 5.1 %slice-start.1 = ((s8[4718592]{0:T(1024)(128)(4,1)}), s8[524288]{0:T(1024)(128)(4,1)S(1)}, s32[]{:S(2)}) async-start(s8[4718592]{0:T(1024)(128)(4,1)} %bitcast.46), calls=%async_computation.4 | async-start | bytes 1048576
  227.3 5.1 %slice-start.5 = ((s8[4718592]{0:T(1024)(128)(4,1)}), s8[524288]{0:T(1024)(128)(4,1)S(1)}, s32[]{:S(2)}) async-start(s8[4718592]{0:T(1024)(128)(4,1)} %bitcast.50), calls=%async_computation.8 | async-start | bytes 1048576
  253.2 10.5 %copy-start.1 = (bf16[2,576,1152]{2,1,0:T(8,128)(2,1)S(1)}, bf16[2,576,1152]{2,1,0:T(8,128)(2,1)}, u32[]{:S(2)}) copy-start(bf16[2,576,1152]{2,1,0:T(8,128)(2,1)} %param.12) | copy-start | bytes 7962628
Sparse Core Ops, SparseCore 0:
  63.6 14.4 all-reduce.10
  80.5 21.5 all-reduce.6
  236.7 14.8 all-reduce.8
where the time goes:
time: 271 us; the launch traced here: 270 us
  blocking collectives  140 us (52%)
  matrix products  53 us (20%)
  other arithmetic  24.3 us (9%)
  waiting for transfers between devices  17.8 us (7%)
  between operations  14.6 us (5%)
  local copies, waits for them, and re-layouts  13.5 us (5%)
  starting transfers between devices  6.99 us (3%)
    unnamed x1, blocking collectives  49 us
    all_gather x1, blocking collectives, body(): normed = lax.all_gather(normed_local, 'feat', axis=1, tiled=True)  44.8 us
    all_gather x1, blocking collectives, body(): errors = lax.all_gather(errors_local, 'feat', axis=0, tiled=True)  43.6 us
    psum x1, waiting for transfers between devices, body(): preact = lax.psum(preact_part, 'mp')  17.4 us
    convert_element_type x1, other arithmetic, body(): grad_decoder = (loss_scale * jnp.stack([outer_product(active_first, error...  16.6 us
    dot_general x3, matrix products, outer_product(): lax.dot_general(weights_side, errors_side, (((0,), (0,)), ((), ())), pref...  15.9 us
    squeeze x1, local copies, waits for them, and re-layouts, body(): decoder[0]  11.3 us
    dot_general x1, matrix products, body(): jnp.einsum('ltd,lfd->tlf', normed, encoder, preferred_element_type=jnp.fl...  8.01 us
  transfers between devices with their start and end apart: 7, of which 2 were waited for; matrix products, arithmetic and copies ran while one was open for 14% of the time, Pallas kernels for 0%

commit v1 on v0

--- a/solution.py
+++ b/solution.py
@@ -6,6 +6,19 @@
 
 D = 2304
 sparsity_weight = 0.1
+
+
+def collect(shard, axis, dim):
+    ways = lax.axis_size(axis)
+    up = [(d, (d + 1) % ways) for d in range(ways)]
+    down = [(d, (d - 1) % ways) for d in range(ways)]
+    earlier, later = ([shard], [shard])
+    for _ in range(ways // 2):
+        earlier.append(lax.ppermute(earlier[-1], axis, up))
+    for _ in range((ways - 1) // 2):
+        later.append(lax.ppermute(later[-1], axis, down))
+    line = jnp.concatenate([*earlier[::-1], *later[1:]], axis=dim)
+    return jnp.roll(line, (lax.axis_index(axis) - ways // 2) * shard.shape[dim], axis=dim)
 
 
 def outer_product(weights_side, errors_side):
@@ -19,7 +32,7 @@
     squares = lax.psum(jnp.sum(values * values, axis=2), "mp")
     inverse_rms = lax.rsqrt(squares / D + 1e-06)
     normed_local = (values * inverse_rms[:, :, None] * norm_gain[:, None, :]).astype(jnp.bfloat16)
-    normed = lax.all_gather(normed_local, "feat", axis=1, tiled=True)
+    normed = collect(normed_local, "feat", 1)
     tokens = normed.shape[1]
     local_rows = residual.shape[1]
     gate_part = jnp.einsum("ltd,ldh->lth", normed, gate_weight, preferred_element_type=jnp.float32)

time: 271 us -> 318 us (1.17)
  blocking collectives: 140 us -> 95.2 us
  starting transfers between devices: 6.99 us -> 48.1 us
  local copies, waits for them, and re-layouts: 13.5 us -> 43.7 us
  waiting for transfers between devices: 17.8 us -> 35.7 us
    all_gather x1 -> x0, blocking collectives: 44.8 us -> none  [body(): normed = lax.all_gather(normed_local, 'feat', axis=1, tiled=True)]
    ppermute x0 -> x15, starting transfers between devices: none -> 41.2 us  [the longest x7 38.3 us: collect(): later.append(lax.ppermute(later[-1], axis, down))]
    concatenate x0 -> x1, local copies, waits for them, and re-layouts: none -> 27.4 us  [collect(): jnp.roll(line, (lax.axis_index(axis) - ways // 2) * shard.shape[dim], axi...]
    ppermute x0 -> x15, waiting for transfers between devices: none -> 17.9 us  [the longest x8 16 us: collect(): earlier.append(lax.ppermute(earlier[-1], axis, up))]
  transfers between devices with their start and end apart: 7 -> 22, of which waited for: 2 -> 17; matrix products, arithmetic and copies ran while one was open for 14% -> 12% of each run, Pallas kernels for 0% -> 0%
where the time goes in v1:
time: 318 us; the launch traced here: 315 us
  blocking collectives  95.2 us (30%)
  matrix products  53.3 us (17%)
  starting transfers between devices  48.1 us (15%)
  local copies, waits for them, and re-layouts  43.7 us (14%)
  waiting for transfers between devices  35.7 us (11%)
  other arithmetic  24.3 us (8%)
  between operations  14.7 us (5%)
    unnamed x1, blocking collectives  49 us
    all_gather x1, blocking collectives, body(): errors = lax.all_gather(errors_local, 'feat', axis=0, tiled=True)  43.6 us
    ppermute x7, starting transfers between devices, collect(): later.append(lax.ppermute(later[-1], axis, down))  38.3 us
    concatenate x1, local copies, waits for them, and re-layouts, collect(): jnp.roll(line, (lax.axis_index(axis) - ways // 2) * shard.shape[dim], axi...  27.4 us
    psum x1, waiting for transfers between devices, body(): preact = lax.psum(preact_part, 'mp')  17.3 us
    convert_element_type x1, other arithmetic, body(): grad_decoder = (loss_scale * jnp.stack([outer_product(active_first, error...  16.6 us
    ppermute x8, waiting for transfers between devices, collect(): earlier.append(lax.ppermute(earlier[-1], axis, up))  16 us
    dot_general x3, matrix products, outer_product(): lax.dot_general(weights_side, errors_side, (((0,), (0,)), ((), ())), pref...  15.9 us
  transfers between devices with their start and end apart: 22, of which 17 were waited for; matrix products, arithmetic and copies ran while one was open for 12% of the time, Pallas kernels for 0%

profile of v1, /device:TPU:0, one launch (start us, length us, event | category | flops | bytes accessed | tf_op | source)
XLA Modules:
  0.0 315.0 jit_solution(17201262854208628063)
XLA Ops:
  7.2 1.0 fusion.38
  8.2 2.6 psum.35
  10.8 0.8 fusion.40
  11.7 2.9 collective-permute-start
  14.5 4.5 %collective-permute-start.8 = (bf16[2,6,1152]{2,1,0:T(8,128)(2,1)S(1)}, bf16[2,6,1152]{2,1,0:T(8,128)(2,1)S(1)}, u32[]{:S(2)}, u32[]{:S(2)}) collective-permute-start(bf16[2,6,1152]{2,1,0:T(8,128)(2,1)S(1)} %fusion.40), channel_id=1, source_target_pairs={{0,15},{1,0},{2,1},{3,2},{4,3},{5,4},{6,5},{7,6},{8,7},{9,8},{10,9... | collective-permute-start | bytes 82952 | tf_op jit(solution)/shard_map/ppermute | solution.py:19
  19.1 1.4 collective-permute-done
  21.1 5.6 %collective-permute-start.9 = (bf16[2,6,1152]{2,1,0:T(8,128)(2,1)S(1)}, bf16[2,6,1152]{2,1,0:T(8,128)(2,1)S(1)}, u32[]{:S(2)}, u32[]{:S(2)}) collective-permute-start(bf16[2,6,1152]{2,1,0:T(8,128)(2,1)S(1)} %collective-permute-done.8), channel_id=1, source_target_pairs={{0,15},{1,0},{2,1},{3,2},{4,3},{5,4},{6,5},{7,6},{8,7},{9,8},{10,9... | collective-permute-start | bytes 82952 | tf_op jit(solution)/shard_map/ppermute | solution.py:19
  26.7 1.4 collective-permute-done.1
  28.6 5.6 %collective-permute-start.10 = (bf16[2,6,1152]{2,1,0:T(8,128)(2,1)S(1)}, bf16[2,6,1152]{2,1,0:T(8,128)(2,1)S(1)}, u32[]{:S(2)}, u32[]{:S(2)}) collective-permute-start(bf16[2,6,1152]{2,1,0:T(8,128)(2,1)S(1)} %collective-permute-done.9), channel_id=1, source_target_pairs={{0,15},{1,0},{2,1},{3,2},{4,3},{5,4},{6,5},{7,6},{8,7},{9,8},{10,9... | collective-permute-start | bytes 82952 | tf_op jit(solution)/shard_map/ppermute | solution.py:19
  34.3 1.3 collective-permute-done.2
  36.2 5.6 %collective-permute-start.11 = (bf16[2,6,1152]{2,1,0:T(8,128)(2,1)S(1)}, bf16[2,6,1152]{2,1,0:T(8,128)(2,1)S(1)}, u32[]{:S(2)}, u32[]{:S(2)}) collective-permute-start(bf16[2,6,1152]{2,1,0:T(8,128)(2,1)S(1)} %collective-permute-done.10), channel_id=1, source_target_pairs={{0,15},{1,0},{2,1},{3,2},{4,3},{5,4},{6,5},{7,6},{8,7},{9,8},{10,9... | collective-permute-start | bytes 82952 | tf_op jit(solution)/shard_map/ppermute | solution.py:19
  41.8 1.3 collective-permute-done.3
  43.8 5.6 %collective-permute-start.12 = (bf16[2,6,1152]{2,1,0:T(8,128)(2,1)S(1)}, bf16[2,6,1152]{2,1,0:T(8,128)(2,1)S(1)}, u32[]{:S(2)}, u32[]{:S(2)}) collective-permute-start(bf16[2,6,1152]{2,1,0:T(8,128)(2,1)S(1)} %collective-permute-done.11), channel_id=1, source_target_pairs={{0,15},{1,0},{2,1},{3,2},{4,3},{5,4},{6,5},{7,6},{8,7},{9,8},{10,9... | collective-permute-start | bytes 82952 | tf_op jit(solution)/shard_map/ppermute | solution.py:19
  49.4 1.3 collective-permute-done.4
  51.3 5.6 %collective-permute-start.13 = (bf16[2,6,1152]{2,1,0:T(8,128)(2,1)S(1)}, bf16[2,6,1152]{2,1,0:T(8,128)(2,1)S(1)}, u32[]{:S(2)}, u32[]{:S(2)}) collective-permute-start(bf16[2,6,1152]{2,1,0:T(8,128)(2,1)S(1)} %collective-permute-done.12), channel_id=1, source_target_pairs={{0,15},{1,0},{2,1},{3,2},{4,3},{5,4},{6,5},{7,6},{8,7},{9,8},{10,9... | collective-permute-start | bytes 82952 | tf_op jit(solution)/shard_map/ppermute | solution.py:19
  56.9 1.6 collective-permute-done.5
  59.1 5.7 %collective-permute-start.14 = (bf16[2,6,1152]{2,1,0:T(8,128)(2,1)S(1)}, bf16[2,6,1152]{2,1,0:T(8,128)(2,1)S(1)}, u32[]{:S(2)}, u32[]{:S(2)}) collective-permute-start(bf16[2,6,1152]{2,1,0:T(8,128)(2,1)S(1)} %collective-permute-done.13), channel_id=1, source_target_pairs={{0,15},{1,0},{2,1},{3,2},{4,3},{5,4},{6,5},{7,6},{8,7},{9,8},{10,9... | collective-permute-start | bytes 82952 | tf_op jit(solution)/shard_map/ppermute | solution.py:19
  64.8 1.3 collective-permute-done.6
  66.7 0.6 copy-done.20
  67.3 6.4 %collective-permute-done.7 = bf16[2,6,1152]{2,1,0:T(8,128)(2,1)} collective-permute-done((bf16[2,6,1152]{2,1,0:T(8,128)(2,1)S(1)}, bf16[2,6,1152]{2,1,0:T(8,128)(2,1)}, u32[]{:S(2)}, u32[]{:S(2)}) %collective-permute-start.7) | collective-permute-done | bytes 27680 | tf_op jit(solution)/shard_map/ppermute | solution.py:17
  73.7 27.4 %concatenate.15 = bf16[2,192,1152]{2,1,0:T(8,128)(2,1)S(1)} concatenate(bf16[2,6,1152]{2,1,0:T(8,128)(2,1)} %collective-permute-done.7, bf16[2,6,1152]{2,1,0:T(8,128)(2,1)} %copy-done.19, bf16[2,6,1152]{2,1,0:T(8,128)(2,1)} %copy-done.17, bf16[2,6,1152]{2,1,0:T(8,128)(2,1)} %copy-done.15, bf16[2,6,1152]{2,1,0:T(8,128)(2,1)} %copy-done.13, bf16[2,6,1152]{2,1,0:T(8,128)(2,1)} %copy-done.11, ...), dimensions={1} | concatenate | bytes 1769472 | tf_op jit(solution)/shard_map/jit(_roll_dynamic)/concatenate | solution.py:21
  101.1 3.7 %convolution_convert_fusion.3 = bf16[2,96,576]{2,1,0:T(8,128)(2,1)} fusion(bf16[2,1152,576]{1,2,0:T(8,128)(2,1)} %param.10, bf16[2,192,1152]{2,1,0:T(8,128)(2,1)S(1)} %concatenate.15, s32[]{:T(128)S(6)} %select_n.18), kind=kOutput, calls=%fused_computation.27 | convolution fusion | flops 254914560 | bytes 3317764 | tf_op jit(solution)/shard_map/ltd,ldh->lth/dot_general | solution.py:38
  104.9 3.4 %convolution_convert_fusion.2 = bf16[2,96,576]{2,1,0:T(8,128)(2,1)} fusion(bf16[2,1152,576]{1,2,0:T(8,128)(2,1)} %param.11, bf16[2,192,1152]{2,1,0:T(8,128)(2,1)S(1)} %concatenate.15, s32[]{:T(128)S(6)} %select_n.18), kind=kOutput, calls=%fused_computation.26 | convolution fusion | flops 254914560 | bytes 3317764 | tf_op jit(solution)/shard_map/ltd,ldh->lth/dot_general | solution.py:39
  108.4 8.0 %convolution_bitcast_fusion.4 = f32[96,2,2048]{2,0,1:T(8,128)} fusion(bf16[2,2048,1152]{2,1,0:T(8,128)(2,1)} %param.13, bf16[2,192,1152]{2,1,0:T(8,128)(2,1)S(1)} %concatenate.15, s32[]{:T(128)S(6)} %select_n.18), kind=kOutput, calls=%fused_computation.18 | convolution fusion | flops 905969664 | bytes 11452420 | tf_op jit(solution)/shard_map/ltd,lfd->tlf/dot_general | solution.py:45
  116.5 11.3 %slice_bitcast_fusion.2 = (bf16[2048,1152]{1,0:T(8,128)(2,1)}, bf16[2048,1152]{1,0:T(8,128)(2,1)}, bf16[2048,1152]{1,0:T(8,128)(2,1)}) fusion(bf16[3,2048,1152]{2,1,0:T(8,128)(2,1)} %param.15), kind=kLoop, calls=%fused_computation.16 | loop fusion | bytes 28311552 | tf_op jit(solution)/shard_map/squeeze | solution.py:56
  127.8 1.7 convolution_bitcast_fusion.3
  129.6 17.3 %all-reduce.7.cloned.1.call-done = f32[96,2,2048]{2,0,1:T(8,128)} async-done(((f32[96,2,2048]{2,0,1:T(8,128)}), f32[96,2,2048]{2,0,1:T(8,128)}) %all-reduce.7.cloned.1.call-update) | async-done | bytes 1572880 | tf_op jit(solution)/shard_map/psum | solution.py:46
  146.9 1.7 maximum_convert_fusion
  148.7 3.7 %fusion.24 = f32[96,1152]{1,0:T(8,128)S(1)} fusion(bf16[96,2,2048]{2,0,1:T(8,128)(2,1)S(1)} %maximum_convert_fusion, bf16[3,2048,1152]{2,1,0:T(8,128)(2,1)} %param.15), kind=kOutput, calls=%fused_computation.43 | convolution fusion | flops 452984832 | bytes 5554176 | tf_op jit(solution)/shard_map/dot_general | solution.py:56
  152.6 0.6 copy-done.4
  153.2 2.0 fusion.2
  155.4 49.0 %fusion = f32[8,2304]{1,0:T(8,128)S(1)} fusion(f32[96,2304]{1,0:T(8,128)S(1)} %maximum_subtract_fusion), kind=kCustom, calls=%all-reduce-scatter | all-reduce-scatter fusion | flops 294913 | bytes 958976
  204.4 1.3 collective-permute-start.16
  205.7 1.3 collective-permute-start.17
  207.0 1.9 collective-permute-start.15
  208.9 2.4 collective-permute-start.18
  211.3 0.6 dynamic-slice.4
  212.9 0.6 concatenate.19
  213.5 43.6 %all-gather = bf16[16,6,2304]{2,1,0:T(8,128)(2,1)S(1)} all-gather(bf16[1,6,2304]{2,1,0:T(8,128)(2,1)S(1)} %fusion.41), channel_id=1, replica_groups=mesh['mp'=2,'feat'=16] {'feat'}, dimensions={0}, use_global_device_ids=true | all-gather | bytes 470016 | tf_op jit(solution)/shard_map/all_gather | solution.py:69
  257.3 3.9 %fusion.16 = bf16[96,1,2048]{2,0,1:T(8,128)(2,1)S(1)} fusion(bf16[96,2304]{1,0:T(8,128)(2,1)S(1)} %reshape.18, bf16[3,2048,1152]{2,1,0:T(8,128)(2,1)} %param.15), kind=kOutput, calls=%fused_computation.22 | convolution fusion | flops 453181440 | bytes 5332992 | tf_op jit(solution)/shard_map/dot_general | solution.py:76
  261.2 5.1 %convolution_bitcast_fusion.1 = f32[1,2048,1152]{2,1,0:T(8,128)} fusion(bf16[96,2,2048]{2,0,1:T(8,128)(2,1)S(1)} %maximum_convert_fusion, bf16[96,2304]{1,0:T(8,128)(2,1)S(1)} %reshape.18), kind=kOutput, calls=%fused_computation.12 | convolution fusion | flops 452984832 | bytes 10051584 | tf_op jit(solution)/shard_map/dot_general | solution.py:25
  266.3 5.8 %convolution_bitcast_fusion = f32[1,2048,1152]{2,1,0:T(8,128)} fusion(bf16[96,2,2048]{2,0,1:T(8,128)(2,1)S(1)} %maximum_convert_fusion, bf16[96,2304]{1,0:T(8,128)(2,1)S(1)} %reshape.18), kind=kOutput, calls=%fused_computation.11 | convolution fusion | flops 452984832 | bytes 10051584 | tf_op jit(solution)/shard_map/dot_general | solution.py:25
  272.1 5.1 %convolution_bitcast_fusion.2 = f32[1,2048,1152]{2,1,0:T(8,128)} fusion(bf16[96,2,2048]{2,0,1:T(8,128)(2,1)S(1)} %maximum_convert_fusion, bf16[96,2304]{1,0:T(8,128)(2,1)S(1)} %reshape.18), kind=kOutput, calls=%fused_computation.13 | convolution fusion | flops 452984832 | bytes 10051584 | tf_op jit(solution)/shard_map/dot_general | solution.py:25
  277.2 3.1 fusion.13
  280.3 1.0 pad_maximum_fusion
  281.3 16.6 %fusion.1 = bf16[3,2048,1152]{2,1,0:T(8,128)(2,1)} fusion(f32[1,2048,1152]{2,1,0:T(8,128)} %convolution_bitcast_fusion, f32[1,2048,1152]{2,1,0:T(8,128)} %convolution_bitcast_fusion.1, f32[1,2048,1152]{2,1,0:T(8,128)} %convolution_bitcast_fusion.2), kind=kLoop, calls=%fused_computation.1 | loop fusion | flops 28311552 | bytes 42467328 | tf_op jit(solution)/shard_map/convert_element_type | solution.py:100
  298.0 2.8 convert_reduce_fusion
  300.8 7.7 %convolution_convert_fusion = bf16[2,2048,1152]{2,1,0:T(8,128)(2,1)} fusion(bf16[2,192,1152]{2,1,0:T(8,128)(2,1)} %copy-done.3, s32[]{:T(128)S(6)} %select_n.18, bf16[96,2,2048]{2,0,1:T(8,128)(2,1)} %all-reduce.9.cloned.1.call-done, bf16[96,2,2048]{2,0,1:T(8,128)(2,1)S(1)} %maximum_convert_fusion), kind=kOutput, calls=%fused_computation.2 | convolution fusion | flops 913047552 | bytes 11452420 | tf_op jit(solution)/shard_map/tlf,ltd->lfd/dot_general | solution.py:85
  (92 shorter events, 5.5 us)
Async XLA Ops:
  7.2 120.6 %copy-start = (bf16[2,576,1152]{2,1,0:T(8,128)(2,1)S(1)}, bf16[2,576,1152]{2,1,0:T(8,128)(2,1)}, u32[]{:S(2)}) copy-start(bf16[2,576,1152]{2,1,0:T(8,128)(2,1)} %param.12) | copy-start | bytes 7962628
  7.2 120.6 %all-reduce.11.cloned.1.call-start = ((), (), s32[]{:S(2)}) async-start(), calls=%async_computation.2 | async-start | bytes 983040 | tf_op jit(solution)/shard_map/psum | solution.py:41
  11.7 2.9 copy-start.5
  11.7 8.8 %collective-permute-start = (bf16[2,6,1152]{2,1,0:T(8,128)(2,1)S(1)}, bf16[2,6,1152]{2,1,0:T(8,128)(2,1)S(1)}, u32[]{:S(2)}, u32[]{:S(2)}) collective-permute-start(bf16[2,6,1152]{2,1,0:T(8,128)(2,1)S(1)} %fusion.40), channel_id=1, source_target_pairs={{0,1},{1,2},{2,3},{3,4},{4,5},{5,6},{6,7},{7,8},{8,9},{9,10},{10,1... | collective-permute-start | bytes 82952 | tf_op jit(solution)/shard_map/ppermute | solution.py:17
  14.5 6.2 %collective-permute-start.8 = (bf16[2,6,1152]{2,1,0:T(8,128)(2,1)S(1)}, bf16[2,6,1152]{2,1,0:T(8,128)(2,1)S(1)}, u32[]{:S(2)}, u32[]{:S(2)}) collective-permute-start(bf16[2,6,1152]{2,1,0:T(8,128)(2,1)S(1)} %fusion.40), channel_id=1, source_target_pairs={{0,15},{1,0},{2,1},{3,2},{4,3},{5,4},{6,5},{7,6},{8,7},{9,8},{10,9... | collective-permute-start | bytes 82952 | tf_op jit(solution)/shard_map/ppermute | solution.py:19
  20.5 0.6 copy-start.7
  20.5 7.6 %collective-permute-start.1 = (bf16[2,6,1152]{2,1,0:T(8,128)(2,1)S(1)}, bf16[2,6,1152]{2,1,0:T(8,128)(2,1)S(1)}, u32[]{:S(2)}, u32[]{:S(2)}) collective-permute-start(bf16[2,6,1152]{2,1,0:T(8,128)(2,1)S(1)} %collective-permute-done), channel_id=1, source_target_pairs={{0,1},{1,2},{2,3},{3,4},{4,5},{5,6},{6,7},{7,8},{8,9},{9,10},{10,1... | collective-permute-start | bytes 82952 | tf_op jit(solution)/shard_map/ppermute | solution.py:17
  21.1 6.9 %copy-start.8 = (bf16[2,6,1152]{2,1,0:T(8,128)(2,1)}, bf16[2,6,1152]{2,1,0:T(8,128)(2,1)S(1)}, u32[]{:S(2)}) copy-start(bf16[2,6,1152]{2,1,0:T(8,128)(2,1)S(1)} %collective-permute-done.8) | copy-start | bytes 82948
  21.1 7.2 %collective-permute-start.9 = (bf16[2,6,1152]{2,1,0:T(8,128)(2,1)S(1)}, bf16[2,6,1152]{2,1,0:T(8,128)(2,1)S(1)}, u32[]{:S(2)}, u32[]{:S(2)}) collective-permute-start(bf16[2,6,1152]{2,1,0:T(8,128)(2,1)S(1)} %collective-permute-done.8), channel_id=1, source_target_pairs={{0,15},{1,0},{2,1},{3,2},{4,3},{5,4},{6,5},{7,6},{8,7},{9,8},{10,9... | collective-permute-start | bytes 82952 | tf_op jit(solution)/shard_map/ppermute | solution.py:19
  28.0 0.6 copy-start.9
  28.0 7.6 %collective-permute-start.2 = (bf16[2,6,1152]{2,1,0:T(8,128)(2,1)S(1)}, bf16[2,6,1152]{2,1,0:T(8,128)(2,1)S(1)}, u32[]{:S(2)}, u32[]{:S(2)}) collective-permute-start(bf16[2,6,1152]{2,1,0:T(8,128)(2,1)S(1)} %collective-permute-done.1), channel_id=1, source_target_pairs={{0,1},{1,2},{2,3},{3,4},{4,5},{5,6},{6,7},{7,8},{8,9},{9,10},{10,1... | collective-permute-start | bytes 82952 | tf_op jit(solution)/shard_map/ppermute | solution.py:17
  28.6 6.9 %copy-start.10 = (bf16[2,6,1152]{2,1,0:T(8,128)(2,1)}, bf16[2,6,1152]{2,1,0:T(8,128)(2,1)S(1)}, u32[]{:S(2)}) copy-start(bf16[2,6,1152]{2,1,0:T(8,128)(2,1)S(1)} %collective-permute-done.9) | copy-start | bytes 82948
  28.6 7.3 %collective-permute-start.10 = (bf16[2,6,1152]{2,1,0:T(8,128)(2,1)S(1)}, bf16[2,6,1152]{2,1,0:T(8,128)(2,1)S(1)}, u32[]{:S(2)}, u32[]{:S(2)}) collective-permute-start(bf16[2,6,1152]{2,1,0:T(8,128)(2,1)S(1)} %collective-permute-done.9), channel_id=1, source_target_pairs={{0,15},{1,0},{2,1},{3,2},{4,3},{5,4},{6,5},{7,6},{8,7},{9,8},{10,9... | collective-permute-start | bytes 82952 | tf_op jit(solution)/shard_map/ppermute | solution.py:19
  35.6 7.6 %collective-permute-start.3 = (bf16[2,6,1152]{2,1,0:T(8,128)(2,1)S(1)}, bf16[2,6,1152]{2,1,0:T(8,128)(2,1)S(1)}, u32[]{:S(2)}, u32[]{:S(2)}) collective-permute-start(bf16[2,6,1152]{2,1,0:T(8,128)(2,1)S(1)} %collective-permute-done.2), channel_id=1, source_target_pairs={{0,1},{1,2},{2,3},{3,4},{4,5},{5,6},{6,7},{7,8},{8,9},{9,10},{10,1... | collective-permute-start | bytes 82952 | tf_op jit(solution)/shard_map/ppermute | solution.py:17
  36.2 7.0 %copy-start.12 = (bf16[2,6,1152]{2,1,0:T(8,128)(2,1)}, bf16[2,6,1152]{2,1,0:T(8,128)(2,1)S(1)}, u32[]{:S(2)}) copy-start(bf16[2,6,1152]{2,1,0:T(8,128)(2,1)S(1)} %collective-permute-done.10) | copy-start | bytes 82948
  36.2 7.3 %collective-permute-start.11 = (bf16[2,6,1152]{2,1,0:T(8,128)(2,1)S(1)}, bf16[2,6,1152]{2,1,0:T(8,128)(2,1)S(1)}, u32[]{:S(2)}, u32[]{:S(2)}) collective-permute-start(bf16[2,6,1152]{2,1,0:T(8,128)(2,1)S(1)} %collective-permute-done.10), channel_id=1, source_target_pairs={{0,15},{1,0},{2,1},{3,2},{4,3},{5,4},{6,5},{7,6},{8,7},{9,8},{10,9... | collective-permute-start | bytes 82952 | tf_op jit(solution)/shard_map/ppermute | solution.py:19
  43.1 0.6 copy-start.13
  43.1 7.6 %collective-permute-start.4 = (bf16[2,6,1152]{2,1,0:T(8,128)(2,1)S(1)}, bf16[2,6,1152]{2,1,0:T(8,128)(2,1)S(1)}, u32[]{:S(2)}, u32[]{:S(2)}) collective-permute-start(bf16[2,6,1152]{2,1,0:T(8,128)(2,1)S(1)} %collective-permute-done.3), channel_id=1, source_target_pairs={{0,1},{1,2},{2,3},{3,4},{4,5},{5,6},{6,7},{7,8},{8,9},{9,10},{10,1... | collective-permute-start | bytes 82952 | tf_op jit(solution)/shard_map/ppermute | solution.py:17
  43.8 6.9 %copy-start.14 = (bf16[2,6,1152]{2,1,0:T(8,128)(2,1)}, bf16[2,6,1152]{2,1,0:T(8,128)(2,1)S(1)}, u32[]{:S(2)}) copy-start(bf16[2,6,1152]{2,1,0:T(8,128)(2,1)S(1)} %collective-permute-done.11) | copy-start | bytes 82948
  43.8 7.3 %collective-permute-start.12 = (bf16[2,6,1152]{2,1,0:T(8,128)(2,1)S(1)}, bf16[2,6,1152]{2,1,0:T(8,128)(2,1)S(1)}, u32[]{:S(2)}, u32[]{:S(2)}) collective-permute-start(bf16[2,6,1152]{2,1,0:T(8,128)(2,1)S(1)} %collective-permute-done.11), channel_id=1, source_target_pairs={{0,15},{1,0},{2,1},{3,2},{4,3},{5,4},{6,5},{7,6},{8,7},{9,8},{10,9... | collective-permute-start | bytes 82952 | tf_op jit(solution)/shard_map/ppermute | solution.py:19
  50.7 7.8 %collective-permute-start.5 = (bf16[2,6,1152]{2,1,0:T(8,128)(2,1)S(1)}, bf16[2,6,1152]{2,1,0:T(8,128)(2,1)S(1)}, u32[]{:S(2)}, u32[]{:S(2)}) collective-permute-start(bf16[2,6,1152]{2,1,0:T(8,128)(2,1)S(1)} %collective-permute-done.4), channel_id=1, source_target_pairs={{0,1},{1,2},{2,3},{3,4},{4,5},{5,6},{6,7},{7,8},{8,9},{9,10},{10,1... | collective-permute-start | bytes 82952 | tf_op jit(solution)/shard_map/ppermute | solution.py:17
  51.3 7.2 %copy-start.16 = (bf16[2,6,1152]{2,1,0:T(8,128)(2,1)}, bf16[2,6,1152]{2,1,0:T(8,128)(2,1)S(1)}, u32[]{:S(2)}) copy-start(bf16[2,6,1152]{2,1,0:T(8,128)(2,1)S(1)} %collective-permute-done.12) | copy-start | bytes 82948
  51.3 7.4 %collective-permute-start.13 = (bf16[2,6,1152]{2,1,0:T(8,128)(2,1)S(1)}, bf16[2,6,1152]{2,1,0:T(8,128)(2,1)S(1)}, u32[]{:S(2)}, u32[]{:S(2)}) collective-permute-start(bf16[2,6,1152]{2,1,0:T(8,128)(2,1)S(1)} %collective-permute-done.12), channel_id=1, source_target_pairs={{0,15},{1,0},{2,1},{3,2},{4,3},{5,4},{6,5},{7,6},{8,7},{9,8},{10,9... | collective-permute-start | bytes 82952 | tf_op jit(solution)/shard_map/ppermute | solution.py:19
  58.5 0.6 copy-start.17
  58.5 7.6 %collective-permute-start.6 = (bf16[2,6,1152]{2,1,0:T(8,128)(2,1)S(1)}, bf16[2,6,1152]{2,1,0:T(8,128)(2,1)S(1)}, u32[]{:S(2)}, u32[]{:S(2)}) collective-permute-start(bf16[2,6,1152]{2,1,0:T(8,128)(2,1)S(1)} %collective-permute-done.5), channel_id=1, source_target_pairs={{0,1},{1,2},{2,3},{3,4},{4,5},{5,6},{6,7},{7,8},{8,9},{9,10},{10,1... | collective-permute-start | bytes 82952 | tf_op jit(solution)/shard_map/ppermute | solution.py:17
  59.1 7.3 %copy-start.18 = (bf16[2,6,1152]{2,1,0:T(8,128)(2,1)}, bf16[2,6,1152]{2,1,0:T(8,128)(2,1)S(1)}, u32[]{:S(2)}) copy-start(bf16[2,6,1152]{2,1,0:T(8,128)(2,1)S(1)} %collective-permute-done.13) | copy-start | bytes 82948
  59.1 7.3 %collective-permute-start.14 = (bf16[2,6,1152]{2,1,0:T(8,128)(2,1)S(1)}, bf16[2,6,1152]{2,1,0:T(8,128)(2,1)S(1)}, u32[]{:S(2)}, u32[]{:S(2)}) collective-permute-start(bf16[2,6,1152]{2,1,0:T(8,128)(2,1)S(1)} %collective-permute-done.13), channel_id=1, source_target_pairs={{0,15},{1,0},{2,1},{3,2},{4,3},{5,4},{6,5},{7,6},{8,7},{9,8},{10,9... | collective-permute-start | bytes 82952 | tf_op jit(solution)/shard_map/ppermute | solution.py:19
  66.1 0.6 copy-start.19
  66.1 7.7 %collective-permute-start.7 = (bf16[2,6,1152]{2,1,0:T(8,128)(2,1)S(1)}, bf16[2,6,1152]{2,1,0:T(8,128)(2,1)}, u32[]{:S(2)}, u32[]{:S(2)}) collective-permute-start(bf16[2,6,1152]{2,1,0:T(8,128)(2,1)S(1)} %collective-permute-done.6), channel_id=1, source_target_pairs={{0,1},{1,2},{2,3},{3,4},{4,5},{5,6},{6,7},{7,8},{8,9},{9,10},{10,1... | collective-permute-start | bytes 82952 | tf_op jit(solution)/shard_map/ppermute | solution.py:17
  66.7 0.6 copy-start.20
  101.1 15.3 %copy-start.3 = (bf16[2,192,1152]{2,1,0:T(8,128)(2,1)}, bf16[2,192,1152]{2,1,0:T(8,128)(2,1)S(1)}, u32[]{:S(2)}) copy-start(bf16[2,192,1152]{2,1,0:T(8,128)(2,1)S(1)} %concatenate.15) | copy-start | bytes 2654212
  108.3 38.6 %all-reduce.7.cloned.1.call-start = ((), (), s32[]{:S(2)}) async-start(), calls=%async_computation | async-start | bytes 3145728 | tf_op jit(solution)/shard_map/psum | solution.py:46
  116.4 181.5 %all-reduce.9.cloned.1.call-start = ((), (), s32[]{:S(2)}) async-start(), calls=%async_computation.1 | async-start | bytes 1572864 | tf_op jit(solution)/shard_map/psum | solution.py:81
  127.8 19.1 %copy-start.6 = (f32[2,2048]{1,0:T(2,128)S(1)}, f32[2,2048]{1,0:T(2,128)}, u32[]{:S(2)}) copy-start(f32[2,2048]{1,0:T(2,128)} %param.14) | copy-start | bytes 49156
  146.9 5.5 %copy-start.2 = (f32[96,2,2048]{2,0,1:T(8,128)S(1)}, f32[96,2,2048]{2,0,1:T(8,128)}, u32[]{:S(2)}) copy-start(f32[96,2,2048]{2,0,1:T(8,128)} %all-reduce.7.cloned.1.call-done) | copy-start | bytes 4718596
  146.9 5.7 %slice-start.2 = ((s8[4718592]{0:T(1024)(128)(4,1)}), s8[4194304]{0:T(1024)(128)(4,1)S(1)}, s32[]{:S(2)}) async-start(s8[4718592]{0:T(1024)(128)(4,1)} %bitcast.48), calls=%async_computation.5 | async-start | bytes 8388608
  148.6 4.0 %slice-start.3 = ((s8[4718592]{0:T(1024)(128)(4,1)}), s8[524288]{0:T(1024)(128)(4,1)S(1)}, s32[]{:S(2)}) async-start(s8[4718592]{0:T(1024)(128)(4,1)} %bitcast.48), calls=%async_computation.6 | async-start | bytes 1048576
  148.6 4.6 %copy-start.4 = (bf16[2048,1152]{1,0:T(8,128)(2,1)S(1)}, bf16[2048,1152]{1,0:T(8,128)(2,1)}, u32[]{:S(2)}) copy-start(bf16[2048,1152]{1,0:T(8,128)(2,1)} %get-tuple-element.6) | copy-start | bytes 14155780
  153.2 58.1 %copy-start.21 = (u32[32]{0:T(128)S(1)}, u32[32]{0:T(128)}, u32[]{:S(2)}) copy-start(u32[32]{0:T(128)} %constant.54) | copy-start | bytes 388
  204.4 8.5 %collective-permute-start.16 = (bf16[8,2304]{1,0:T(8,128)(2,1)S(1)}, bf16[8,2304]{1,0:T(8,128)(2,1)S(1)}, u32[]{:S(2)}, u32[]{:S(2)}) collective-permute-start(bf16[8,2304]{1,0:T(8,128)(2,1)S(1)} %convert.22), channel_id=1, source_target_pairs={{0,2},{1,3},{2,4},{3,5},{4,6},{5,7},{6,8},{7,9},{8,10},{9,11},{10,... | collective-permute-start | bytes 110600
  205.7 7.2 %collective-permute-start.17 = (bf16[8,2304]{1,0:T(8,128)(2,1)S(1)}, bf16[8,2304]{1,0:T(8,128)(2,1)S(1)}, u32[]{:S(2)}, u32[]{:S(2)}) collective-permute-start(bf16[8,2304]{1,0:T(8,128)(2,1)S(1)} %convert.22), channel_id=1, source_target_pairs={{0,3},{1,4},{2,5},{3,6},{4,7},{5,8},{6,9},{7,10},{8,11},{9,12},{10... | collective-permute-start | bytes 110600
  207.0 5.9 %collective-permute-start.15 = (bf16[8,2304]{1,0:T(8,128)(2,1)S(1)}, bf16[8,2304]{1,0:T(8,128)(2,1)S(1)}, u32[]{:S(2)}, u32[]{:S(2)}) collective-permute-start(bf16[8,2304]{1,0:T(8,128)(2,1)S(1)} %convert.22), channel_id=1, source_target_pairs={{0,1},{1,2},{2,3},{3,4},{4,5},{5,6},{6,7},{7,8},{8,9},{9,10},{10,1... | collective-permute-start | bytes 110600
  208.9 4.0 %collective-permute-start.18 = (bf16[6,2304]{1,0:T(8,128)(2,1)S(1)}, bf16[6,2304]{1,0:T(8,128)(2,1)S(1)}, u32[]{:S(2)}, u32[]{:S(2)}) collective-permute-start(bf16[6,2304]{1,0:T(8,128)(2,1)S(1)} %slice.36), channel_id=1, source_target_pairs={{0,4},{1,5},{2,6},{3,7},{4,8},{5,9},{6,10},{7,11},{8,12},{9,13},{1... | collective-permute-start | bytes 82952
  266.3 10.9 %slice-start = ((s8[4718592]{0:T(1024)(128)(4,1)}), s8[4194304]{0:T(1024)(128)(4,1)S(1)}, s32[]{:S(2)}) async-start(s8[4718592]{0:T(1024)(128)(4,1)} %bitcast.46), calls=%async_computation.3 | async-start | bytes 8388608
  266.3 10.9 %slice-start.4 = ((s8[4718592]{0:T(1024)(128)(4,1)}), s8[4194304]{0:T(1024)(128)(4,1)S(1)}, s32[]{:S(2)}) async-start(s8[4718592]{0:T(1024)(128)(4,1)} %bitcast.50), calls=%async_computation.7 | async-start | bytes 8388608
  272.1 5.1 %slice-start.1 = ((s8[4718592]{0:T(1024)(128)(4,1)}), s8[524288]{0:T(1024)(128)(4,1)S(1)}, s32[]{:S(2)}) async-start(s8[4718592]{0:T(1024)(128)(4,1)} %bitcast.46), calls=%async_computation.4 | async-start | bytes 1048576
  272.1 5.1 %slice-start.5 = ((s8[4718592]{0:T(1024)(128)(4,1)}), s8[524288]{0:T(1024)(128)(4,1)S(1)}, s32[]{:S(2)}) async-start(s8[4718592]{0:T(1024)(128)(4,1)} %bitcast.50), calls=%async_computation.8 | async-start | bytes 1048576
  298.0 10.5 %copy-start.1 = (bf16[2,576,1152]{2,1,0:T(8,128)(2,1)S(1)}, bf16[2,576,1152]{2,1,0:T(8,128)(2,1)}, u32[]{:S(2)}) copy-start(bf16[2,576,1152]{2,1,0:T(8,128)(2,1)} %param.12) | copy-start | bytes 7962628
  (2 other events, 1.2 us)
Sparse Core Ops, SparseCore 0:
  108.4 14.4 all-reduce.10
  125.3 21.5 all-reduce.6
  281.4 14.8 all-reduce.8
